TPU v7x, 256 devices: a whole 4x4x8 slice. The times are simulated.
256 devices in a mesh: depth: 32 (over z, x_hi, core), shot: 8 (over y, x_lo).
Axes of the slice: x: 4 (x_hi: 2, x_lo: 2; x = x_hi * 2 + x_lo), y: 4, z: 8, core: 2. Of those that a mesh axis runs over, the one named last changes fastest.
Arguments:
- courant: float32 [512, 64, 128], P('depth'), may hold values from 0.04 to 0.2
- wave_before: float32 [8, 512, 64, 128], P('shot', 'depth'), may hold values from -10 to 10
- wave_current: float32 [8, 512, 64, 128], P('shot', 'depth'), may hold values from -10 to 10
- adjoint_after: float32 [8, 512, 64, 128], P('shot', 'depth'), may hold values from -10 to 10
- adjoint_current: float32 [8, 512, 64, 128], P('shot', 'depth'), may hold values from -10 to 10
- source_cell: int32 [8], P('shot'), may hold values from 0 to 4194303
- wavelet: float32 [8, 4], P('shot'), may hold values from -15 to 15
- receiver_cell: int32 [8, 256], P('shot'), may hold values from 0 to 4194303
- residual: float32 [8, 4, 256], P('shot'), may hold values from -12 to 12
- history: float32 [2, 5, 512, 64, 128], P(None, None, 'depth', 'shot'), may hold values from -23 to 23, as said below
Outputs:
- gradient: float32 [512, 64, 128], P('depth', 'shot')
- direction: float32 [512, 64, 128], P('depth', 'shot')
- courant_next: float32 [512, 64, 128], P('depth')
Inputs may be any that keep to these rules, and one draw needn't show every extreme that they name: In every pair the sum over all cells of history[0] times history[1] is positive.
All inputs are finite; a program needn't handle non-finite values.
Results may differ from a plain program's by a relative error of at most 0.00026.
Values sent between devices are 32-bit elements; how exact they have to be, the bound alone decides.
A program may use at most 128 MiB of HBM per device.

v0:
```python
import jax
import jax.numpy as jnp
from jax import lax
from jax.sharding import PartitionSpec as P

STEPS = 4
PAIRS = 5
coefficients = (-205.0 / 72.0, 8.0 / 5.0, -1.0 / 5.0, 8.0 / 315.0, -1.0 / 560.0)


def with_halo(cells, sides, width):
    for axis, dim in sides:
        count = lax.axis_size(axis)
        ends = count - 1
        head = lax.slice_in_dim(cells, 0, width, axis=dim)
        tail = lax.slice_in_dim(cells, cells.shape[dim] - width, cells.shape[dim], axis=dim)
        cells = jnp.concatenate(
            [
                lax.ppermute(tail, axis, [(i, (i + 1) % count) for i in range(ends)]),
                cells,
                lax.ppermute(head, axis, [((i + 1) % count, i) for i in range(ends)]),
            ],
            axis=dim,
        )
    return cells


def laplace_core(extended):
    interior = extended[4:-4]
    count_rows = interior.shape[0]
    width_x = interior.shape[1]
    width_y = interior.shape[2]
    padded = jnp.pad(interior, ((0, 0), (4, 4), (4, 4)))
    summed = 3.0 * coefficients[0] * interior
    for reach in range(1, 5):
        weight = coefficients[reach]
        summed = summed + weight * (
            extended[4 + reach : 4 + reach + count_rows]
            + extended[4 - reach : 4 - reach + count_rows]
        )
        summed = summed + weight * (
            padded[:, 4 + reach : 4 + reach + width_x, 4 : 4 + width_y]
            + padded[:, 4 - reach : 4 - reach + width_x, 4 : 4 + width_y]
        )
        summed = summed + weight * (
            padded[:, 4 : 4 + width_x, 4 + reach : 4 + reach + width_y]
            + padded[:, 4 : 4 + width_x, 4 - reach : 4 - reach + width_y]
        )
    return summed


def inject(volume, cell_ids, values, offset):
    count_rows = volume.shape[0]
    plane_size = volume.shape[1] * volume.shape[2]
    depth_row = cell_ids // plane_size - offset
    remainder = cell_ids % plane_size
    inside = (depth_row >= 0) & (depth_row < count_rows)
    row_safe = jnp.clip(depth_row, 0, count_rows - 1)
    return volume.at[row_safe, remainder // volume.shape[2], remainder % volume.shape[2]].add(
        jnp.where(inside, values, jnp.zeros_like(values))
    )


def per_device(
    courant,
    wave_before,
    wave_current,
    adjoint_after,
    adjoint_current,
    source_cell,
    wavelet,
    receiver_cell,
    residual,
    history,
):
    slab_rows = courant.shape[0]
    first_row = lax.axis_index("depth") * slab_rows
    shot_count = lax.axis_size("shot")
    summed = jnp.zeros(courant.shape, jnp.float32)
    laplacians = []
    wave_old = wave_before[0]
    wave_now = wave_current[0]
    for moment in range(STEPS):
        extended = with_halo(wave_now, (("depth", 0),), 4)
        laplacian = laplace_core(extended)
        wave_new = 2.0 * wave_now - wave_old + courant * laplacian
        wave_new = inject(wave_new, source_cell, wavelet[0, moment : moment + 1], first_row)
        laplacians.append(laplacian)
        wave_old, wave_now = (wave_now, wave_new)
    adjoint_old = adjoint_after[0]
    adjoint_now = adjoint_current[0]
    for moment in reversed(range(STEPS)):
        extended = with_halo(courant * adjoint_now, (("depth", 0),), 4)
        adjoint_new = 2.0 * adjoint_now - adjoint_old + laplace_core(extended)
        adjoint_new = inject(adjoint_new, receiver_cell[0], residual[0, moment], first_row)
        summed = summed + adjoint_new * laplacians[moment]
        adjoint_old, adjoint_now = (adjoint_now, adjoint_new)
    grad_piece = lax.psum_scatter(summed, "shot", scatter_dimension=1, tiled=True) * (
        1.0 / (shot_count * STEPS)
    )
    displaced = history[0]
    changes = history[1]
    step_change = jnp.einsum("izxy,jzxy->ij", displaced, changes, precision=lax.Precision.HIGHEST)
    change_change = jnp.einsum("izxy,jzxy->ij", changes, changes, precision=lax.Precision.HIGHEST)
    step_grad = jnp.sum(displaced * grad_piece, axis=(1, 2, 3))
    change_grad = jnp.sum(changes * grad_piece, axis=(1, 2, 3))
    packed = jnp.concatenate(
        [step_change, change_change, step_grad[None], change_grad[None]], axis=0
    )
    packed = lax.psum(packed, ("depth", "shot"))
    step_change = packed[:PAIRS]
    change_change = packed[PAIRS : 2 * PAIRS]
    step_grad = packed[2 * PAIRS]
    change_grad = packed[2 * PAIRS + 1]
    inverse = [1.0 / step_change[i, i] for i in range(PAIRS)]
    alphas = [None] * PAIRS
    for i in reversed(range(PAIRS)):
        value = step_grad[i]
        for j in range(i + 1, PAIRS):
            value = value - alphas[j] * step_change[i, j]
        alphas[i] = inverse[i] * value
    gamma = step_change[PAIRS - 1, PAIRS - 1] / change_change[PAIRS - 1, PAIRS - 1]
    gains = []
    for i in range(PAIRS):
        value = change_grad[i]
        for j in range(PAIRS):
            value = value - alphas[j] * change_change[i, j]
        value = gamma * value
        for j in range(i):
            value = value + gains[j] * step_change[j, i]
        gains.append(alphas[i] - inverse[i] * value)
    scaled = grad_piece
    for i in range(PAIRS):
        scaled = scaled - alphas[i] * changes[i]
    scaled = gamma * scaled
    for i in range(PAIRS):
        scaled = scaled + gains[i] * displaced[i]
    direction = -scaled
    piece_width = grad_piece.shape[1]
    own_courant = lax.dynamic_slice_in_dim(
        courant, lax.axis_index("shot") * piece_width, piece_width, 1
    )
    next_piece = own_courant + 0.05 * direction
    courant_next = lax.all_gather(next_piece, "shot", axis=1, tiled=True)
    return (grad_piece, direction, courant_next)


def solution(mesh):
    return jax.shard_map(
        per_device,
        mesh=mesh,
        in_specs=(
            P("depth", None, None),
            P("shot", "depth", None, None),
            P("shot", "depth", None, None),
            P("shot", "depth", None, None),
            P("shot", "depth", None, None),
            P("shot"),
            P("shot", None),
            P("shot", None),
            P("shot", None, None),
            P(None, None, "depth", "shot", None),
        ),
        out_specs=(P("depth", "shot", None), P("depth", "shot", None), P("depth", None, None)),
        check_vma=False,
    )
```

profile of v0, /device:TPU:32, one launch (start us, length us, event | category | flops | bytes accessed | tf_op | source)
XLA Modules:
  0.0 397.9 jit_solution(11437620847095359479)
XLA Ops:
  7.2 1.3 bitcast_multiply_fusion
  8.6 4.0 %collective-permute-start = (f32[4,64,128]{2,1,0:T(8,128)S(1)}, f32[4,64,128]{2,1,0:T(8,128)S(1)}, u32[]{:S(2)}, u32[]{:S(2)}) collective-permute-start(f32[4,64,128]{2,1,0:T(8,128)S(1)} %get-tuple-element.70), channel_id=1, source_target_pairs={{8,0},{16,8},{24,16},{32,24},{40,32},{48,40},{56,48},{64,56},{72,6... | collective-permute-start | bytes 393224 | tf_op jit(solution)/shard_map/ppermute | solution.py:21
  12.7 1.9 collective-permute-start.1
  14.7 6.0 %collective-permute-start.2 = (f32[4,64,128]{2,1,0:T(8,128)S(1)}, f32[4,64,128]{2,1,0:T(8,128)S(1)}, u32[]{:S(2)}, u32[]{:S(2)}) collective-permute-start(f32[4,64,128]{2,1,0:T(8,128)S(1)} %get-tuple-element.68), channel_id=1, source_target_pairs={{8,0},{16,8},{24,16},{32,24},{40,32},{48,40},{56,48},{64,56},{72,6... | collective-permute-start | bytes 393224 | tf_op jit(solution)/shard_map/ppermute | solution.py:21
  20.7 1.9 collective-permute-start.3
  23.3 0.7 fusion.369
  26.7 0.7 and_reduce_fusion
  27.4 1.9 fusion.184
  29.4 23.9 %scatter_fusion = f32[16,64,128]{2,1,0:T(8,128)S(1)} fusion(f32[16,64,128]{2,1,0:T(8,128)S(1)} %fusion.184, s32[256]{0:T(256)S(1)} %bitcast.180, f32[256]{0:T(256)} %get-tuple-element.128), kind=kCustom, calls=%fused_computation | custom fusion | flops 256 | bytes 6144 | tf_op jit(solution)/shard_map/scatter-add | solution.py:59
  53.4 3.7 fusion.348
  57.0 0.7 dynamic-slice.24
  59.8 6.1 %collective-permute-start.10 = (f32[4,64,128]{2,1,0:T(8,128)S(1)}, f32[4,64,128]{2,1,0:T(8,128)S(1)}, u32[]{:S(2)}, u32[]{:S(2)}) collective-permute-start(f32[4,64,128]{2,1,0:T(8,128)S(1)} %get-tuple-element.59), channel_id=1, source_target_pairs={{8,0},{16,8},{24,16},{32,24},{40,32},{48,40},{56,48},{64,56},{72,6... | collective-permute-start | bytes 393224 | tf_op jit(solution)/shard_map/ppermute | solution.py:21
  65.9 1.9 collective-permute-start.11
  67.8 0.7 fusion.363
  68.5 6.0 %collective-permute-start.4 = (f32[4,64,128]{2,1,0:T(8,128)}, f32[4,64,128]{2,1,0:T(8,128)S(1)}, u32[]{:S(2)}, u32[]{:S(2)}) collective-permute-start(f32[4,64,128]{2,1,0:T(8,128)} %get-tuple-element.66), channel_id=1, source_target_pairs={{8,0},{16,8},{24,16},{32,24},{40,32},{48,40},{56,48},{64,56},{72,6... | collective-permute-start | bytes 393224 | tf_op jit(solution)/shard_map/ppermute | solution.py:21
  74.5 1.9 collective-permute-start.5
  76.5 9.1 %fusion.59 = f32[16,64,128]{2,1,0:T(8,128)S(1)} fusion(f32[16,64,128]{2,1,0:T(8,128)} %copy-done.6, f32[4,64,128]{2,1,0:T(8,128)S(1)} %collective-permute-done.11, f32[4,64,128]{2,1,0:T(8,128)S(1)} %collective-permute-done.10, f32[1,16,64,128]{3,2,1,0:T(8,128)S(1)} %copy-done.2, f32[16,64,128]{2,1,0:T(8,128)S(1)} %scatter_fusion), kind=kLoop, calls=%fused_computation.289 | loop fusion | flops 6291456 | bytes 2359296 | tf_op jit(solution)/shard_map/add | solution.py:94
  85.6 15.2 %scatter_fusion.1 = f32[16,64,128]{2,1,0:T(8,128)S(1)} fusion(f32[16,64,128]{2,1,0:T(8,128)S(1)} %fusion.59, s32[256]{0:T(256)S(1)} %bitcast.181, f32[256]{0:T(256)S(1)} %get-tuple-element.127), kind=kCustom, calls=%fused_computation.1 | custom fusion | flops 256 | bytes 6144 | tf_op jit(solution)/shard_map/scatter-add | solution.py:59
  100.9 2.7 multiply_add_fusion.1
  103.6 6.1 %collective-permute-start.12 = (f32[4,64,128]{2,1,0:T(8,128)S(1)}, f32[4,64,128]{2,1,0:T(8,128)S(1)}, u32[]{:S(2)}, u32[]{:S(2)}) collective-permute-start(f32[4,64,128]{2,1,0:T(8,128)S(1)} %get-tuple-element.56), channel_id=1, source_target_pairs={{8,0},{16,8},{24,16},{32,24},{40,32},{48,40},{56,48},{64,56},{72,6... | collective-permute-start | bytes 393224 | tf_op jit(solution)/shard_map/ppermute | solution.py:21
  109.7 1.9 collective-permute-start.13
  111.6 0.6 dynamic-slice.25
  114.3 0.7 fusion.362
  115.0 6.0 %collective-permute-start.6 = (f32[4,64,128]{2,1,0:T(8,128)}, f32[4,64,128]{2,1,0:T(8,128)S(1)}, u32[]{:S(2)}, u32[]{:S(2)}) collective-permute-start(f32[4,64,128]{2,1,0:T(8,128)} %get-tuple-element.64), channel_id=1, source_target_pairs={{8,0},{16,8},{24,16},{32,24},{40,32},{48,40},{56,48},{64,56},{72,6... | collective-permute-start | bytes 393224 | tf_op jit(solution)/shard_map/ppermute | solution.py:21
  121.1 1.9 collective-permute-start.7
  123.0 2.0 fusion.34
  125.0 15.2 %scatter_fusion.2 = f32[16,64,128]{2,1,0:T(8,128)S(1)} fusion(f32[16,64,128]{2,1,0:T(8,128)S(1)} %fusion.34, s32[256]{0:T(256)S(1)} %bitcast.182, f32[256]{0:T(256)S(1)} %get-tuple-element.126), kind=kCustom, calls=%fused_computation.2 | custom fusion | flops 256 | bytes 6144 | tf_op jit(solution)/shard_map/scatter-add | solution.py:59
  140.2 10.6 %multiply_add_fusion = (f32[16,64,128]{2,1,0:T(8,128)S(1)}, f32[16,64,128]{2,1,0:T(8,128)}, f32[16,64,128]{2,1,0:T(8,128)S(1)}) fusion(f32[16,64,128]{2,1,0:T(8,128)S(1)} %copy-done, f32[16,64,128]{2,1,0:T(8,128)S(1)} %scatter-add.44, f32[16,64,128]{2,1,0:T(8,128)} %copy-done.3, f32[4,64,128]{2,1,0:T(8,128)} %collective-permute-done.7, ...), kind=kLoop, calls=%fused_computation.602 | loop fusion | flops 6553600 | bytes 3932160 | tf_op jit(solution)/shard_map/add | solution.py:86
  150.9 6.1 %collective-permute-start.14 = (f32[4,64,128]{2,1,0:T(8,128)S(1)}, f32[4,64,128]{2,1,0:T(8,128)S(1)}, u32[]{:S(2)}, u32[]{:S(2)}) collective-permute-start(f32[4,64,128]{2,1,0:T(8,128)S(1)} %get-tuple-element.53), channel_id=1, source_target_pairs={{8,0},{16,8},{24,16},{32,24},{40,32},{48,40},{56,48},{64,56},{72,6... | collective-permute-start | bytes 393224 | tf_op jit(solution)/shard_map/ppermute | solution.py:21
  156.9 2.1 collective-permute-start.15
  161.7 0.7 fusion.361
  162.4 6.0 %collective-permute-start.8 = (f32[4,64,128]{2,1,0:T(8,128)}, f32[4,64,128]{2,1,0:T(8,128)S(1)}, u32[]{:S(2)}, u32[]{:S(2)}) collective-permute-start(f32[4,64,128]{2,1,0:T(8,128)} %get-tuple-element.62), channel_id=1, source_target_pairs={{8,0},{16,8},{24,16},{32,24},{40,32},{48,40},{56,48},{64,56},{72,6... | collective-permute-start | bytes 393224 | tf_op jit(solution)/shard_map/ppermute | solution.py:21
  168.5 1.9 collective-permute-start.9
  170.4 2.2 fusion.9
  172.7 15.2 %scatter_fusion.3 = f32[16,64,128]{2,1,0:T(8,128)S(1)} fusion(f32[16,64,128]{2,1,0:T(8,128)S(1)} %fusion.9, s32[256]{0:T(256)S(1)} %bitcast.183, f32[256]{0:T(256)S(1)} %get-tuple-element.43), kind=kCustom, calls=%fused_computation.3 | custom fusion | flops 256 | bytes 6144 | tf_op jit(solution)/shard_map/scatter-add | solution.py:59
  187.9 3.9 fusion.87
  191.9 1.1 fusion.357
  193.0 1.2 convolution_bitcast_fusion
  194.2 1.4 convolution_bitcast_fusion.1
  195.6 48.2 %reduce-scatter.2.cloned.1.call-done = f32[16,8,128]{2,1,0:T(8,128)} async-done(((f32[16,64,128]{2,1,0:T(8,128)}), f32[16,8,128]{2,1,0:T(8,128)}) %reduce-scatter.2.cloned.1.call-update) | async-done | bytes 65552 | tf_op jit(solution)/shard_map/reduce_scatter | solution.py:98
  243.7 0.8 broadcast_multiply_fusion
  245.4 73.3 %psum.7 = f32[12,5]{0,1:T(8,128)S(1)} all-reduce(f32[12,5]{0,1:T(8,128)S(1)} %pad_maximum_fusion.16), channel_id=1, replica_groups=mesh['depth'=32,'shot'=8] {'depth','shot'}, use_global_device_ids=true, to_apply=%region_8.9 | all-reduce | flops 60 | bytes 480 | tf_op jit(solution)/shard_map/psum | solution.py:110
  318.8 0.7 fusion.366
  319.5 0.7 fusion.367
  320.2 0.7 fusion.365
  359.7 0.7 multiply_add_fusion.2
  360.4 29.8 %all_gather.3 = f32[16,64,128]{2,1,0:T(8,128)S(1)} all-gather(f32[16,8,128]{2,1,0:T(8,128)S(1)} %get-tuple-element.41), channel_id=1, replica_groups=mesh['depth'=32,'shot'=8] {'shot'}, dimensions={1}, use_global_device_ids=true | all-gather | bytes 589824 | tf_op jit(solution)/shard_map/all_gather | solution.py:144
  390.3 0.8 copy.49
  (70 shorter events, 2.7 us)
Async XLA Ops:
  7.2 236.6 %reduce-scatter.2.cloned.1.call-start = ((), (), s32[]{:S(2)}) async-start(), calls=%async_computation.1 | async-start | bytes 589824 | tf_op jit(solution)/shard_map/reduce_scatter | solution.py:98
  7.2 20.2 %copy-start.10 = (f32[1,16,64,128]{3,2,1,0:T(8,128)S(1)}, f32[1,16,64,128]{3,2,1,0:T(8,128)}, u32[]{:S(2)}) copy-start(f32[1,16,64,128]{3,2,1,0:T(8,128)} %param.19) | copy-start | bytes 1572868
  8.5 6.1 %copy-start.1 = (f32[1,16,64,128]{3,2,1,0:T(8,128)S(1)}, f32[1,16,64,128]{3,2,1,0:T(8,128)}, u32[]{:S(2)}) copy-start(f32[1,16,64,128]{3,2,1,0:T(8,128)} %param.18) | copy-start | bytes 1572868
  8.6 14.1 %copy-start.14 = (f32[1,4,256]{2,1,0:T(4,128)S(1)}, f32[1,4,256]{2,1,0:T(4,128)}, u32[]{:S(2)}) copy-start(f32[1,4,256]{2,1,0:T(4,128)} %param.24) | copy-start | bytes 12292
  8.6 14.1 %copy-start.15 = (s32[1,256]{1,0:T(1,128)S(1)}, s32[1,256]{1,0:T(1,128)}, u32[]{:S(2)}) copy-start(s32[1,256]{1,0:T(1,128)} %param.23) | copy-start | bytes 3076
  8.6 14.7 %copy-start.13 = (f32[1,4]{1,0:T(1,128)S(1)}, f32[1,4]{1,0:T(1,128)}, u32[]{:S(2)}) copy-start(f32[1,4]{1,0:T(1,128)} %param.22) | copy-start | bytes 52
  8.6 18.1 %copy-start.16 = (s32[3]{0:T(128)S(1)}, s32[3]{0:T(128)}, u32[]{:S(2)}) copy-start(s32[3]{0:T(128)} %constant.255.clone.1) | copy-start | bytes 40
  8.6 18.8 %copy-start.2 = (f32[1,16,64,128]{3,2,1,0:T(8,128)S(1)}, f32[1,16,64,128]{3,2,1,0:T(8,128)}, u32[]{:S(2)}) copy-start(f32[1,16,64,128]{3,2,1,0:T(8,128)} %param.20) | copy-start | bytes 1572868
  8.6 18.8 %collective-permute-start = (f32[4,64,128]{2,1,0:T(8,128)S(1)}, f32[4,64,128]{2,1,0:T(8,128)S(1)}, u32[]{:S(2)}, u32[]{:S(2)}) collective-permute-start(f32[4,64,128]{2,1,0:T(8,128)S(1)} %get-tuple-element.70), channel_id=1, source_target_pairs={{8,0},{16,8},{24,16},{32,24},{40,32},{48,40},{56,48},{64,56},{72,6... | collective-permute-start | bytes 393224 | tf_op jit(solution)/shard_map/ppermute | solution.py:21
  12.7 14.7 %collective-permute-start.1 = (f32[4,64,128]{2,1,0:T(8,128)S(1)}, f32[4,64,128]{2,1,0:T(8,128)S(1)}, u32[]{:S(2)}, u32[]{:S(2)}) collective-permute-start(f32[4,64,128]{2,1,0:T(8,128)S(1)} %get-tuple-element.71), channel_id=1, source_target_pairs={{0,8},{8,16},{16,24},{24,32},{32,40},{40,48},{48,56},{56,64},{64,7... | collective-permute-start | bytes 393224 | tf_op jit(solution)/shard_map/ppermute | solution.py:19
  14.7 38.7 %collective-permute-start.2 = (f32[4,64,128]{2,1,0:T(8,128)S(1)}, f32[4,64,128]{2,1,0:T(8,128)S(1)}, u32[]{:S(2)}, u32[]{:S(2)}) collective-permute-start(f32[4,64,128]{2,1,0:T(8,128)S(1)} %get-tuple-element.68), channel_id=1, source_target_pairs={{8,0},{16,8},{24,16},{32,24},{40,32},{48,40},{56,48},{64,56},{72,6... | collective-permute-start | bytes 393224 | tf_op jit(solution)/shard_map/ppermute | solution.py:21
  20.7 32.6 %collective-permute-start.3 = (f32[4,64,128]{2,1,0:T(8,128)S(1)}, f32[4,64,128]{2,1,0:T(8,128)S(1)}, u32[]{:S(2)}, u32[]{:S(2)}) collective-permute-start(f32[4,64,128]{2,1,0:T(8,128)S(1)} %get-tuple-element.69), channel_id=1, source_target_pairs={{0,8},{8,16},{16,24},{24,32},{32,40},{40,48},{48,56},{56,64},{64,7... | collective-permute-start | bytes 393224 | tf_op jit(solution)/shard_map/ppermute | solution.py:19
  29.4 24.0 %copy-start = (f32[16,64,128]{2,1,0:T(8,128)S(1)}, f32[16,64,128]{2,1,0:T(8,128)}, u32[]{:S(2)}) copy-start(f32[16,64,128]{2,1,0:T(8,128)} %param.16) | copy-start | bytes 1572868
  57.0 19.4 %copy-start.6 = (f32[16,64,128]{2,1,0:T(8,128)}, f32[16,64,128]{2,1,0:T(8,128)S(1)}, u32[]{:S(2)}) copy-start(f32[16,64,128]{2,1,0:T(8,128)S(1)} %get-tuple-element.61) | copy-start | bytes 1572868
  59.8 16.6 %collective-permute-start.10 = (f32[4,64,128]{2,1,0:T(8,128)S(1)}, f32[4,64,128]{2,1,0:T(8,128)S(1)}, u32[]{:S(2)}, u32[]{:S(2)}) collective-permute-start(f32[4,64,128]{2,1,0:T(8,128)S(1)} %get-tuple-element.59), channel_id=1, source_target_pairs={{8,0},{16,8},{24,16},{32,24},{40,32},{48,40},{56,48},{64,56},{72,6... | collective-permute-start | bytes 393224 | tf_op jit(solution)/shard_map/ppermute | solution.py:21
  65.9 10.6 %collective-permute-start.11 = (f32[4,64,128]{2,1,0:T(8,128)S(1)}, f32[4,64,128]{2,1,0:T(8,128)S(1)}, u32[]{:S(2)}, u32[]{:S(2)}) collective-permute-start(f32[4,64,128]{2,1,0:T(8,128)S(1)} %get-tuple-element.60), channel_id=1, source_target_pairs={{0,8},{8,16},{16,24},{24,32},{32,40},{40,48},{48,56},{56,64},{64,7... | collective-permute-start | bytes 393224 | tf_op jit(solution)/shard_map/ppermute | solution.py:19
  68.5 32.4 %collective-permute-start.4 = (f32[4,64,128]{2,1,0:T(8,128)}, f32[4,64,128]{2,1,0:T(8,128)S(1)}, u32[]{:S(2)}, u32[]{:S(2)}) collective-permute-start(f32[4,64,128]{2,1,0:T(8,128)} %get-tuple-element.66), channel_id=1, source_target_pairs={{8,0},{16,8},{24,16},{32,24},{40,32},{48,40},{56,48},{64,56},{72,6... | collective-permute-start | bytes 393224 | tf_op jit(solution)/shard_map/ppermute | solution.py:21
  74.5 26.3 %collective-permute-start.5 = (f32[4,64,128]{2,1,0:T(8,128)S(1)}, f32[4,64,128]{2,1,0:T(8,128)S(1)}, u32[]{:S(2)}, u32[]{:S(2)}) collective-permute-start(f32[4,64,128]{2,1,0:T(8,128)S(1)} %get-tuple-element.67), channel_id=1, source_target_pairs={{0,8},{8,16},{16,24},{24,32},{32,40},{40,48},{48,56},{56,64},{64,7... | collective-permute-start | bytes 393224 | tf_op jit(solution)/shard_map/ppermute | solution.py:19
  103.6 9.3 %copy-start.7 = (f32[16,64,128]{2,1,0:T(8,128)}, f32[16,64,128]{2,1,0:T(8,128)S(1)}, u32[]{:S(2)}) copy-start(f32[16,64,128]{2,1,0:T(8,128)S(1)} %get-tuple-element.58) | copy-start | bytes 1572868
  103.6 19.4 %collective-permute-start.12 = (f32[4,64,128]{2,1,0:T(8,128)S(1)}, f32[4,64,128]{2,1,0:T(8,128)S(1)}, u32[]{:S(2)}, u32[]{:S(2)}) collective-permute-start(f32[4,64,128]{2,1,0:T(8,128)S(1)} %get-tuple-element.56), channel_id=1, source_target_pairs={{8,0},{16,8},{24,16},{32,24},{40,32},{48,40},{56,48},{64,56},{72,6... | collective-permute-start | bytes 393224 | tf_op jit(solution)/shard_map/ppermute | solution.py:21
  109.7 13.3 %collective-permute-start.13 = (f32[4,64,128]{2,1,0:T(8,128)S(1)}, f32[4,64,128]{2,1,0:T(8,128)S(1)}, u32[]{:S(2)}, u32[]{:S(2)}) collective-permute-start(f32[4,64,128]{2,1,0:T(8,128)S(1)} %get-tuple-element.57), channel_id=1, source_target_pairs={{0,8},{8,16},{16,24},{24,32},{32,40},{40,48},{48,56},{56,64},{64,7... | collective-permute-start | bytes 393224 | tf_op jit(solution)/shard_map/ppermute | solution.py:19
  114.3 10.7 %copy-start.3 = (f32[16,64,128]{2,1,0:T(8,128)}, f32[16,64,128]{2,1,0:T(8,128)S(1)}, u32[]{:S(2)}) copy-start(f32[16,64,128]{2,1,0:T(8,128)S(1)} %scatter-add.45) | copy-start | bytes 1572868
  114.3 8.7 %copy-start.8 = (f32[16,64,128]{2,1,0:T(8,128)S(1)}, f32[16,64,128]{2,1,0:T(8,128)}, u32[]{:S(2)}) copy-start(f32[16,64,128]{2,1,0:T(8,128)} %copy-done.7) | copy-start | bytes 1572868
  115.0 25.2 %collective-permute-start.6 = (f32[4,64,128]{2,1,0:T(8,128)}, f32[4,64,128]{2,1,0:T(8,128)S(1)}, u32[]{:S(2)}, u32[]{:S(2)}) collective-permute-start(f32[4,64,128]{2,1,0:T(8,128)} %get-tuple-element.64), channel_id=1, source_target_pairs={{8,0},{16,8},{24,16},{32,24},{40,32},{48,40},{56,48},{64,56},{72,6... | collective-permute-start | bytes 393224 | tf_op jit(solution)/shard_map/ppermute | solution.py:21
  121.1 19.2 %collective-permute-start.7 = (f32[4,64,128]{2,1,0:T(8,128)}, f32[4,64,128]{2,1,0:T(8,128)}, u32[]{:S(2)}, u32[]{:S(2)}) collective-permute-start(f32[4,64,128]{2,1,0:T(8,128)} %get-tuple-element.65), channel_id=1, source_target_pairs={{0,8},{8,16},{16,24},{24,32},{32,40},{40,48},{48,56},{56,64},{64,7... | collective-permute-start | bytes 393224 | tf_op jit(solution)/shard_map/ppermute | solution.py:19
  150.8 9.5 %copy-start.4 = (f32[16,64,128]{2,1,0:T(8,128)}, f32[16,64,128]{2,1,0:T(8,128)S(1)}, u32[]{:S(2)}) copy-start(f32[16,64,128]{2,1,0:T(8,128)S(1)} %get-tuple-element.55) | copy-start | bytes 1572868
  150.9 19.6 %collective-permute-start.14 = (f32[4,64,128]{2,1,0:T(8,128)S(1)}, f32[4,64,128]{2,1,0:T(8,128)S(1)}, u32[]{:S(2)}, u32[]{:S(2)}) collective-permute-start(f32[4,64,128]{2,1,0:T(8,128)S(1)} %get-tuple-element.53), channel_id=1, source_target_pairs={{8,0},{16,8},{24,16},{32,24},{40,32},{48,40},{56,48},{64,56},{72,6... | collective-permute-start | bytes 393224 | tf_op jit(solution)/shard_map/ppermute | solution.py:21
  156.9 13.5 %collective-permute-start.15 = (f32[4,64,128]{2,1,0:T(8,128)S(1)}, f32[4,64,128]{2,1,0:T(8,128)}, u32[]{:S(2)}, u32[]{:S(2)}) collective-permute-start(f32[4,64,128]{2,1,0:T(8,128)S(1)} %get-tuple-element.54), channel_id=1, source_target_pairs={{0,8},{8,16},{16,24},{24,32},{32,40},{40,48},{48,56},{56,64},{64,7... | collective-permute-start | bytes 393224 | tf_op jit(solution)/shard_map/ppermute | solution.py:19
  161.7 8.7 %copy-start.5 = (f32[16,64,128]{2,1,0:T(8,128)S(1)}, f32[16,64,128]{2,1,0:T(8,128)}, u32[]{:S(2)}) copy-start(f32[16,64,128]{2,1,0:T(8,128)} %copy-done.4) | copy-start | bytes 1572868
  162.4 25.5 %collective-permute-start.8 = (f32[4,64,128]{2,1,0:T(8,128)}, f32[4,64,128]{2,1,0:T(8,128)S(1)}, u32[]{:S(2)}, u32[]{:S(2)}) collective-permute-start(f32[4,64,128]{2,1,0:T(8,128)} %get-tuple-element.62), channel_id=1, source_target_pairs={{8,0},{16,8},{24,16},{32,24},{40,32},{48,40},{56,48},{64,56},{72,6... | collective-permute-start | bytes 393224 | tf_op jit(solution)/shard_map/ppermute | solution.py:21
  168.5 19.4 %collective-permute-start.9 = (f32[4,64,128]{2,1,0:T(8,128)}, f32[4,64,128]{2,1,0:T(8,128)S(1)}, u32[]{:S(2)}, u32[]{:S(2)}) collective-permute-start(f32[4,64,128]{2,1,0:T(8,128)} %get-tuple-element.63), channel_id=1, source_target_pairs={{0,8},{8,16},{16,24},{24,32},{32,40},{40,48},{48,56},{56,64},{64,7... | collective-permute-start | bytes 393224 | tf_op jit(solution)/shard_map/ppermute | solution.py:19
  244.6 111.4 %copy-start.12 = (f32[16,8,128]{2,1,0:T(8,128)}, f32[16,8,128]{2,1,0:T(8,128)S(1)}, u32[]{:S(2)}) copy-start(f32[16,8,128]{2,1,0:T(8,128)S(1)} %broadcast_multiply_fusion) | copy-start | bytes 196612
  244.6 115.1 %copy-start.9 = (f32[2,5,16,8,128]{4,3,2,1,0:T(8,128)S(1)}, f32[2,5,16,8,128]{4,3,2,1,0:T(8,128)}, u32[]{:S(2)}) copy-start(f32[2,5,16,8,128]{4,3,2,1,0:T(8,128)} %param.25) | copy-start | bytes 1966084
  244.6 115.1 %copy-start.11 = (f32[16,8,128]{2,1,0:T(8,128)S(1)}, f32[16,8,128]{2,1,0:T(8,128)}, u32[]{:S(2)}) copy-start(f32[16,8,128]{2,1,0:T(8,128)} %reduce-scatter.2.cloned.1.call-done) | copy-start | bytes 196612
Sparse Core Ops, SparseCore 0:
  192.0 51.6 reduce-scatter.1
where the time goes:
time: 400 us; the launch traced here: 398 us
  other arithmetic  111 us (28%)
  blocking collectives  103 us (26%)
  starting transfers between devices  61.9 us (15%)
  between operations  61.9 us (15%)
  waiting for transfers between devices  48.2 us (12%)
  local copies, waits for them, and re-layouts  9.48 us (2%)
    psum x1, blocking collectives, per_device(): packed = lax.psum(packed, ('depth', 'shot'))  73.3 us
    scatter-add x4, other arithmetic, inject(): volume.at[row_safe, remainder // volume.shape[2], remainder % volume.shap...  69.6 us
    reduce_scatter x1, waiting for transfers between devices, per_device(): lax.psum_scatter(summed, 'shot', scatter_dimension=1, tiled=True)  48.2 us
    ppermute x8, starting transfers between devices, with_halo(): lax.ppermute(head, axis, [((i + 1) % count, i) for i in range(ends)])  46.4 us
    all_gather x1, blocking collectives, per_device(): courant_next = lax.all_gather(next_piece, 'shot', axis=1, tiled=True)  29.8 us
    add x3, other arithmetic, per_device(): wave_new = 2.0 * wave_now - wave_old + courant * laplacian  17 us
    ppermute x8, starting transfers between devices, with_halo(): lax.ppermute(tail, axis, [(i, (i + 1) % count) for i in range(ends)])  15.5 us
    add x4, other arithmetic, per_device(): adjoint_new = 2.0 * adjoint_now - adjoint_old + laplace_core(extended)  15.3 us
  transfers between devices with their start and end apart: 17, of which 1 were waited for; matrix products, arithmetic and copies ran while one was open for 24% of the time, Pallas kernels for 0%

commit v1 on v0

--- a/solution.py
+++ b/solution.py
@@ -107,7 +107,7 @@
     packed = jnp.concatenate(
         [step_change, change_change, step_grad[None], change_grad[None]], axis=0
     )
-    packed = lax.psum(packed, ("depth", "shot"))
+    packed = lax.psum(lax.psum(packed, "shot"), "depth")
     step_change = packed[:PAIRS]
     change_change = packed[PAIRS : 2 * PAIRS]
     step_grad = packed[2 * PAIRS]

time: 400 us -> 406 us (1.015)
  the two profiles are of different devices: /device:TPU:32 before, /device:TPU:0 now
where the time goes in v1:
time: 406 us; the launch traced here: 405 us
  blocking collectives  112 us (28%)
  other arithmetic  110 us (27%)
  between operations  61.9 us (15%)
  waiting for transfers between devices  55.9 us (14%)
  starting transfers between devices  52.9 us (13%)
  local copies, waits for them, and re-layouts  9.43 us (2%)
    psum x2, blocking collectives, per_device(): packed = lax.psum(lax.psum(packed, 'shot'), 'depth')  81.8 us
    scatter-add x4, other arithmetic, inject(): volume.at[row_safe, remainder // volume.shape[2], remainder % volume.shap...  69.7 us
    reduce_scatter x1, waiting for transfers between devices, per_device(): lax.psum_scatter(summed, 'shot', scatter_dimension=1, tiled=True)  55.8 us
    ppermute x8, starting transfers between devices, with_halo(): lax.ppermute(tail, axis, [(i, (i + 1) % count) for i in range(ends)])  42.4 us
    all_gather x1, blocking collectives, per_device(): courant_next = lax.all_gather(next_piece, 'shot', axis=1, tiled=True)  29.9 us
    add x3, other arithmetic, per_device(): wave_new = 2.0 * wave_now - wave_old + courant * laplacian  16.5 us
    add x4, other arithmetic, per_device(): adjoint_new = 2.0 * adjoint_now - adjoint_old + laplace_core(extended)  15.2 us
    ppermute x8, starting transfers between devices, with_halo(): lax.ppermute(head, axis, [((i + 1) % count, i) for i in range(ends)])  10.4 us
  transfers between devices with their start and end apart: 17, of which 1 were waited for; matrix products, arithmetic and copies ran while one was open for 23% of the time, Pallas kernels for 0%

profile of v1, /device:TPU:0, one launch (start us, length us, event | category | flops | bytes accessed | tf_op | source)
XLA Modules:
  0.0 404.5 jit_solution(11233957375234092933)
XLA Ops:
  7.2 1.3 bitcast_multiply_fusion
  8.6 1.4 collective-permute-start
  10.1 3.0 collective-permute-start.1
  13.2 1.3 collective-permute-start.2
  14.5 3.4 collective-permute-start.3
  21.8 0.7 and_reduce_fusion
  22.5 1.9 fusion.184
  24.5 24.0 %scatter_fusion = f32[16,64,128]{2,1,0:T(8,128)S(1)} fusion(f32[16,64,128]{2,1,0:T(8,128)S(1)} %fusion.184, s32[256]{0:T(256)S(1)} %bitcast.180, f32[256]{0:T(256)} %get-tuple-element.128), kind=kCustom, calls=%fused_computation | custom fusion | flops 256 | bytes 6144 | tf_op jit(solution)/shard_map/scatter-add | solution.py:59
  48.5 3.7 fusion.348
  52.2 0.7 dynamic-slice.24
  54.9 1.3 collective-permute-start.10
  56.2 5.8 %collective-permute-start.11 = (f32[4,64,128]{2,1,0:T(8,128)S(1)}, f32[4,64,128]{2,1,0:T(8,128)S(1)}, u32[]{:S(2)}, u32[]{:S(2)}) collective-permute-start(f32[4,64,128]{2,1,0:T(8,128)S(1)} %get-tuple-element.60), channel_id=1, source_target_pairs={{0,8},{8,16},{16,24},{24,32},{32,40},{40,48},{48,56},{56,64},{64,7... | collective-permute-start | bytes 393224 | tf_op jit(solution)/shard_map/ppermute | solution.py:19
  62.0 0.7 fusion.363
  62.7 1.3 collective-permute-start.4
  64.0 5.8 %collective-permute-start.5 = (f32[4,64,128]{2,1,0:T(8,128)S(1)}, f32[4,64,128]{2,1,0:T(8,128)S(1)}, u32[]{:S(2)}, u32[]{:S(2)}) collective-permute-start(f32[4,64,128]{2,1,0:T(8,128)S(1)} %get-tuple-element.67), channel_id=1, source_target_pairs={{0,8},{8,16},{16,24},{24,32},{32,40},{40,48},{48,56},{56,64},{64,7... | collective-permute-start | bytes 393224 | tf_op jit(solution)/shard_map/ppermute | solution.py:19
  69.8 9.1 %fusion.59 = f32[16,64,128]{2,1,0:T(8,128)S(1)} fusion(f32[16,64,128]{2,1,0:T(8,128)} %copy-done.6, f32[4,64,128]{2,1,0:T(8,128)S(1)} %collective-permute-done.11, f32[4,64,128]{2,1,0:T(8,128)S(1)} %collective-permute-done.10, f32[1,16,64,128]{3,2,1,0:T(8,128)S(1)} %copy-done.2, f32[16,64,128]{2,1,0:T(8,128)S(1)} %scatter_fusion), kind=kLoop, calls=%fused_computation.289 | loop fusion | flops 6291456 | bytes 2359296 | tf_op jit(solution)/shard_map/add | solution.py:94
  78.9 15.2 %scatter_fusion.1 = f32[16,64,128]{2,1,0:T(8,128)S(1)} fusion(f32[16,64,128]{2,1,0:T(8,128)S(1)} %fusion.59, s32[256]{0:T(256)S(1)} %bitcast.181, f32[256]{0:T(256)S(1)} %get-tuple-element.127), kind=kCustom, calls=%fused_computation.1 | custom fusion | flops 256 | bytes 6144 | tf_op jit(solution)/shard_map/scatter-add | solution.py:59
  94.2 2.7 multiply_add_fusion.1
  96.9 1.3 collective-permute-start.12
  98.2 5.8 %collective-permute-start.13 = (f32[4,64,128]{2,1,0:T(8,128)S(1)}, f32[4,64,128]{2,1,0:T(8,128)S(1)}, u32[]{:S(2)}, u32[]{:S(2)}) collective-permute-start(f32[4,64,128]{2,1,0:T(8,128)S(1)} %get-tuple-element.57), channel_id=1, source_target_pairs={{0,8},{8,16},{16,24},{24,32},{32,40},{40,48},{48,56},{56,64},{64,7... | collective-permute-start | bytes 393224 | tf_op jit(solution)/shard_map/ppermute | solution.py:19
  104.0 0.6 dynamic-slice.25
  106.7 0.7 fusion.362
  107.4 1.3 collective-permute-start.6
  108.7 6.4 %collective-permute-start.7 = (f32[4,64,128]{2,1,0:T(8,128)}, f32[4,64,128]{2,1,0:T(8,128)}, u32[]{:S(2)}, u32[]{:S(2)}) collective-permute-start(f32[4,64,128]{2,1,0:T(8,128)} %get-tuple-element.65), channel_id=1, source_target_pairs={{0,8},{8,16},{16,24},{24,32},{32,40},{40,48},{48,56},{56,64},{64,7... | collective-permute-start | bytes 393224 | tf_op jit(solution)/shard_map/ppermute | solution.py:19
  115.1 2.0 fusion.34
  117.1 15.2 %scatter_fusion.2 = f32[16,64,128]{2,1,0:T(8,128)S(1)} fusion(f32[16,64,128]{2,1,0:T(8,128)S(1)} %fusion.34, s32[256]{0:T(256)S(1)} %bitcast.182, f32[256]{0:T(256)S(1)} %get-tuple-element.126), kind=kCustom, calls=%fused_computation.2 | custom fusion | flops 256 | bytes 6144 | tf_op jit(solution)/shard_map/scatter-add | solution.py:59
  132.4 10.1 %multiply_add_fusion = (f32[16,64,128]{2,1,0:T(8,128)S(1)}, f32[16,64,128]{2,1,0:T(8,128)}, f32[16,64,128]{2,1,0:T(8,128)S(1)}) fusion(f32[16,64,128]{2,1,0:T(8,128)S(1)} %copy-done, f32[16,64,128]{2,1,0:T(8,128)S(1)} %scatter-add.44, f32[16,64,128]{2,1,0:T(8,128)} %copy-done.3, f32[4,64,128]{2,1,0:T(8,128)} %collective-permute-done.7, ...), kind=kLoop, calls=%fused_computation.602 | loop fusion | flops 6553600 | bytes 3932160 | tf_op jit(solution)/shard_map/add | solution.py:86
  142.6 1.3 collective-permute-start.14
  143.9 6.0 %collective-permute-start.15 = (f32[4,64,128]{2,1,0:T(8,128)S(1)}, f32[4,64,128]{2,1,0:T(8,128)}, u32[]{:S(2)}, u32[]{:S(2)}) collective-permute-start(f32[4,64,128]{2,1,0:T(8,128)S(1)} %get-tuple-element.54), channel_id=1, source_target_pairs={{0,8},{8,16},{16,24},{24,32},{32,40},{40,48},{48,56},{56,64},{64,7... | collective-permute-start | bytes 393224 | tf_op jit(solution)/shard_map/ppermute | solution.py:19
  152.5 0.7 fusion.361
  153.2 1.3 collective-permute-start.8
  154.5 6.2 %collective-permute-start.9 = (f32[4,64,128]{2,1,0:T(8,128)}, f32[4,64,128]{2,1,0:T(8,128)S(1)}, u32[]{:S(2)}, u32[]{:S(2)}) collective-permute-start(f32[4,64,128]{2,1,0:T(8,128)} %get-tuple-element.63), channel_id=1, source_target_pairs={{0,8},{8,16},{16,24},{24,32},{32,40},{40,48},{48,56},{56,64},{64,7... | collective-permute-start | bytes 393224 | tf_op jit(solution)/shard_map/ppermute | solution.py:19
  160.8 2.2 fusion.9
  163.0 15.2 %scatter_fusion.3 = f32[16,64,128]{2,1,0:T(8,128)S(1)} fusion(f32[16,64,128]{2,1,0:T(8,128)S(1)} %fusion.9, s32[256]{0:T(256)S(1)} %bitcast.183, f32[256]{0:T(256)S(1)} %get-tuple-element.43), kind=kCustom, calls=%fused_computation.3 | custom fusion | flops 256 | bytes 6144 | tf_op jit(solution)/shard_map/scatter-add | solution.py:59
  178.3 3.9 fusion.87
  182.2 1.1 fusion.357
  183.4 1.2 convolution_bitcast_fusion
  184.6 1.4 convolution_bitcast_fusion.1
  185.9 55.8 %reduce-scatter.2.cloned.1.call-done = f32[16,8,128]{2,1,0:T(8,128)} async-done(((f32[16,64,128]{2,1,0:T(8,128)}), f32[16,8,128]{2,1,0:T(8,128)}) %reduce-scatter.2.cloned.1.call-update) | async-done | bytes 65552 | tf_op jit(solution)/shard_map/reduce_scatter | solution.py:98
  241.8 0.8 broadcast_multiply_fusion
  243.4 16.8 %psum.14 = f32[12,5]{0,1:T(8,128)S(1)} all-reduce(f32[12,5]{0,1:T(8,128)S(1)} %pad_maximum_fusion.16), channel_id=1, replica_groups=mesh['depth'=32,'shot'=8] {'shot'}, use_global_device_ids=true, to_apply=%region_8.9 | all-reduce | flops 60 | bytes 480 | tf_op jit(solution)/shard_map/psum | solution.py:110
  260.2 65.0 %psum.15 = f32[12,5]{0,1:T(8,128)S(1)} all-reduce(f32[12,5]{0,1:T(8,128)S(1)} %psum.14), channel_id=1, replica_groups=mesh['depth'=32,'shot'=8] {'depth'}, use_global_device_ids=true, to_apply=%region_9.10 | all-reduce | flops 60 | bytes 480 | tf_op jit(solution)/shard_map/psum | solution.py:110
  325.3 0.7 fusion.366
  326.0 0.7 fusion.367
  326.7 0.7 fusion.365
  366.3 0.7 multiply_add_fusion.2
  367.0 29.9 %all_gather.3 = f32[16,64,128]{2,1,0:T(8,128)S(1)} all-gather(f32[16,8,128]{2,1,0:T(8,128)S(1)} %get-tuple-element.41), channel_id=1, replica_groups=mesh['depth'=32,'shot'=8] {'shot'}, dimensions={1}, use_global_device_ids=true | all-gather | bytes 589824 | tf_op jit(solution)/shard_map/all_gather | solution.py:144
  396.9 0.8 copy.49
  (71 shorter events, 3.3 us)
Async XLA Ops:
  7.2 234.6 %reduce-scatter.2.cloned.1.call-start = ((), (), s32[]{:S(2)}) async-start(), calls=%async_computation.1 | async-start | bytes 589824 | tf_op jit(solution)/shard_map/reduce_scatter | solution.py:98
  7.2 15.3 %copy-start.10 = (f32[1,16,64,128]{3,2,1,0:T(8,128)S(1)}, f32[1,16,64,128]{3,2,1,0:T(8,128)}, u32[]{:S(2)}) copy-start(f32[1,16,64,128]{3,2,1,0:T(8,128)} %param.19) | copy-start | bytes 1572868
  8.5 4.6 %copy-start.1 = (f32[1,16,64,128]{3,2,1,0:T(8,128)S(1)}, f32[1,16,64,128]{3,2,1,0:T(8,128)}, u32[]{:S(2)}) copy-start(f32[1,16,64,128]{3,2,1,0:T(8,128)} %param.18) | copy-start | bytes 1572868
  8.6 9.4 %copy-start.14 = (f32[1,4,256]{2,1,0:T(4,128)S(1)}, f32[1,4,256]{2,1,0:T(4,128)}, u32[]{:S(2)}) copy-start(f32[1,4,256]{2,1,0:T(4,128)} %param.24) | copy-start | bytes 12292
  8.6 9.4 %copy-start.15 = (s32[1,256]{1,0:T(1,128)S(1)}, s32[1,256]{1,0:T(1,128)}, u32[]{:S(2)}) copy-start(s32[1,256]{1,0:T(1,128)} %param.23) | copy-start | bytes 3076
  8.6 10.0 %copy-start.13 = (f32[1,4]{1,0:T(1,128)S(1)}, f32[1,4]{1,0:T(1,128)}, u32[]{:S(2)}) copy-start(f32[1,4]{1,0:T(1,128)} %param.22) | copy-start | bytes 52
  8.6 13.2 %copy-start.16 = (s32[3]{0:T(128)S(1)}, s32[3]{0:T(128)}, u32[]{:S(2)}) copy-start(s32[3]{0:T(128)} %constant.255.clone.1) | copy-start | bytes 40
  8.6 13.9 %copy-start.2 = (f32[1,16,64,128]{3,2,1,0:T(8,128)S(1)}, f32[1,16,64,128]{3,2,1,0:T(8,128)}, u32[]{:S(2)}) copy-start(f32[1,16,64,128]{3,2,1,0:T(8,128)} %param.20) | copy-start | bytes 1572868
  8.6 13.9 %collective-permute-start = (f32[4,64,128]{2,1,0:T(8,128)S(1)}, f32[4,64,128]{2,1,0:T(8,128)S(1)}, u32[]{:S(2)}, u32[]{:S(2)}) collective-permute-start(f32[4,64,128]{2,1,0:T(8,128)S(1)} %get-tuple-element.70), channel_id=1, source_target_pairs={{8,0},{16,8},{24,16},{32,24},{40,32},{48,40},{56,48},{64,56},{72,6... | collective-permute-start | bytes 393224 | tf_op jit(solution)/shard_map/ppermute | solution.py:21
  10.1 12.4 %collective-permute-start.1 = (f32[4,64,128]{2,1,0:T(8,128)S(1)}, f32[4,64,128]{2,1,0:T(8,128)S(1)}, u32[]{:S(2)}, u32[]{:S(2)}) collective-permute-start(f32[4,64,128]{2,1,0:T(8,128)S(1)} %get-tuple-element.71), channel_id=1, source_target_pairs={{0,8},{8,16},{16,24},{24,32},{32,40},{40,48},{48,56},{56,64},{64,7... | collective-permute-start | bytes 393224 | tf_op jit(solution)/shard_map/ppermute | solution.py:19
  13.2 35.3 %collective-permute-start.2 = (f32[4,64,128]{2,1,0:T(8,128)S(1)}, f32[4,64,128]{2,1,0:T(8,128)S(1)}, u32[]{:S(2)}, u32[]{:S(2)}) collective-permute-start(f32[4,64,128]{2,1,0:T(8,128)S(1)} %get-tuple-element.68), channel_id=1, source_target_pairs={{8,0},{16,8},{24,16},{32,24},{40,32},{48,40},{56,48},{64,56},{72,6... | collective-permute-start | bytes 393224 | tf_op jit(solution)/shard_map/ppermute | solution.py:21
  14.5 34.0 %collective-permute-start.3 = (f32[4,64,128]{2,1,0:T(8,128)S(1)}, f32[4,64,128]{2,1,0:T(8,128)S(1)}, u32[]{:S(2)}, u32[]{:S(2)}) collective-permute-start(f32[4,64,128]{2,1,0:T(8,128)S(1)} %get-tuple-element.69), channel_id=1, source_target_pairs={{0,8},{8,16},{16,24},{24,32},{32,40},{40,48},{48,56},{56,64},{64,7... | collective-permute-start | bytes 393224 | tf_op jit(solution)/shard_map/ppermute | solution.py:19
  24.5 24.0 %copy-start = (f32[16,64,128]{2,1,0:T(8,128)S(1)}, f32[16,64,128]{2,1,0:T(8,128)}, u32[]{:S(2)}) copy-start(f32[16,64,128]{2,1,0:T(8,128)} %param.16) | copy-start | bytes 1572868
  52.2 17.6 %copy-start.6 = (f32[16,64,128]{2,1,0:T(8,128)}, f32[16,64,128]{2,1,0:T(8,128)S(1)}, u32[]{:S(2)}) copy-start(f32[16,64,128]{2,1,0:T(8,128)S(1)} %get-tuple-element.61) | copy-start | bytes 1572868
  54.9 14.8 %collective-permute-start.10 = (f32[4,64,128]{2,1,0:T(8,128)S(1)}, f32[4,64,128]{2,1,0:T(8,128)S(1)}, u32[]{:S(2)}, u32[]{:S(2)}) collective-permute-start(f32[4,64,128]{2,1,0:T(8,128)S(1)} %get-tuple-element.59), channel_id=1, source_target_pairs={{8,0},{16,8},{24,16},{32,24},{40,32},{48,40},{56,48},{64,56},{72,6... | collective-permute-start | bytes 393224 | tf_op jit(solution)/shard_map/ppermute | solution.py:21
  56.2 13.5 %collective-permute-start.11 = (f32[4,64,128]{2,1,0:T(8,128)S(1)}, f32[4,64,128]{2,1,0:T(8,128)S(1)}, u32[]{:S(2)}, u32[]{:S(2)}) collective-permute-start(f32[4,64,128]{2,1,0:T(8,128)S(1)} %get-tuple-element.60), channel_id=1, source_target_pairs={{0,8},{8,16},{16,24},{24,32},{32,40},{40,48},{48,56},{56,64},{64,7... | collective-permute-start | bytes 393224 | tf_op jit(solution)/shard_map/ppermute | solution.py:19
  62.7 31.5 %collective-permute-start.4 = (f32[4,64,128]{2,1,0:T(8,128)}, f32[4,64,128]{2,1,0:T(8,128)S(1)}, u32[]{:S(2)}, u32[]{:S(2)}) collective-permute-start(f32[4,64,128]{2,1,0:T(8,128)} %get-tuple-element.66), channel_id=1, source_target_pairs={{8,0},{16,8},{24,16},{32,24},{40,32},{48,40},{56,48},{64,56},{72,6... | collective-permute-start | bytes 393224 | tf_op jit(solution)/shard_map/ppermute | solution.py:21
  64.0 30.2 %collective-permute-start.5 = (f32[4,64,128]{2,1,0:T(8,128)S(1)}, f32[4,64,128]{2,1,0:T(8,128)S(1)}, u32[]{:S(2)}, u32[]{:S(2)}) collective-permute-start(f32[4,64,128]{2,1,0:T(8,128)S(1)} %get-tuple-element.67), channel_id=1, source_target_pairs={{0,8},{8,16},{16,24},{24,32},{32,40},{40,48},{48,56},{56,64},{64,7... | collective-permute-start | bytes 393224 | tf_op jit(solution)/shard_map/ppermute | solution.py:19
  96.9 8.3 %copy-start.7 = (f32[16,64,128]{2,1,0:T(8,128)}, f32[16,64,128]{2,1,0:T(8,128)S(1)}, u32[]{:S(2)}) copy-start(f32[16,64,128]{2,1,0:T(8,128)S(1)} %get-tuple-element.58) | copy-start | bytes 1572868
  96.9 18.2 %collective-permute-start.12 = (f32[4,64,128]{2,1,0:T(8,128)S(1)}, f32[4,64,128]{2,1,0:T(8,128)S(1)}, u32[]{:S(2)}, u32[]{:S(2)}) collective-permute-start(f32[4,64,128]{2,1,0:T(8,128)S(1)} %get-tuple-element.56), channel_id=1, source_target_pairs={{8,0},{16,8},{24,16},{32,24},{40,32},{48,40},{56,48},{64,56},{72,6... | collective-permute-start | bytes 393224 | tf_op jit(solution)/shard_map/ppermute | solution.py:21
  98.2 16.9 %collective-permute-start.13 = (f32[4,64,128]{2,1,0:T(8,128)S(1)}, f32[4,64,128]{2,1,0:T(8,128)S(1)}, u32[]{:S(2)}, u32[]{:S(2)}) collective-permute-start(f32[4,64,128]{2,1,0:T(8,128)S(1)} %get-tuple-element.57), channel_id=1, source_target_pairs={{0,8},{8,16},{16,24},{24,32},{32,40},{40,48},{48,56},{56,64},{64,7... | collective-permute-start | bytes 393224 | tf_op jit(solution)/shard_map/ppermute | solution.py:19
  106.7 10.4 %copy-start.3 = (f32[16,64,128]{2,1,0:T(8,128)}, f32[16,64,128]{2,1,0:T(8,128)S(1)}, u32[]{:S(2)}) copy-start(f32[16,64,128]{2,1,0:T(8,128)S(1)} %scatter-add.45) | copy-start | bytes 1572868
  106.7 8.4 %copy-start.8 = (f32[16,64,128]{2,1,0:T(8,128)S(1)}, f32[16,64,128]{2,1,0:T(8,128)}, u32[]{:S(2)}) copy-start(f32[16,64,128]{2,1,0:T(8,128)} %copy-done.7) | copy-start | bytes 1572868
  107.4 25.0 %collective-permute-start.6 = (f32[4,64,128]{2,1,0:T(8,128)}, f32[4,64,128]{2,1,0:T(8,128)S(1)}, u32[]{:S(2)}, u32[]{:S(2)}) collective-permute-start(f32[4,64,128]{2,1,0:T(8,128)} %get-tuple-element.64), channel_id=1, source_target_pairs={{8,0},{16,8},{24,16},{32,24},{40,32},{48,40},{56,48},{64,56},{72,6... | collective-permute-start | bytes 393224 | tf_op jit(solution)/shard_map/ppermute | solution.py:21
  108.7 23.7 %collective-permute-start.7 = (f32[4,64,128]{2,1,0:T(8,128)}, f32[4,64,128]{2,1,0:T(8,128)}, u32[]{:S(2)}, u32[]{:S(2)}) collective-permute-start(f32[4,64,128]{2,1,0:T(8,128)} %get-tuple-element.65), channel_id=1, source_target_pairs={{0,8},{8,16},{16,24},{24,32},{32,40},{40,48},{48,56},{56,64},{64,7... | collective-permute-start | bytes 393224 | tf_op jit(solution)/shard_map/ppermute | solution.py:19
  142.5 8.5 %copy-start.4 = (f32[16,64,128]{2,1,0:T(8,128)}, f32[16,64,128]{2,1,0:T(8,128)S(1)}, u32[]{:S(2)}) copy-start(f32[16,64,128]{2,1,0:T(8,128)S(1)} %get-tuple-element.55) | copy-start | bytes 1572868
  142.6 18.2 %collective-permute-start.14 = (f32[4,64,128]{2,1,0:T(8,128)S(1)}, f32[4,64,128]{2,1,0:T(8,128)S(1)}, u32[]{:S(2)}, u32[]{:S(2)}) collective-permute-start(f32[4,64,128]{2,1,0:T(8,128)S(1)} %get-tuple-element.53), channel_id=1, source_target_pairs={{8,0},{16,8},{24,16},{32,24},{40,32},{48,40},{56,48},{64,56},{72,6... | collective-permute-start | bytes 393224 | tf_op jit(solution)/shard_map/ppermute | solution.py:21
  143.9 16.9 %collective-permute-start.15 = (f32[4,64,128]{2,1,0:T(8,128)S(1)}, f32[4,64,128]{2,1,0:T(8,128)}, u32[]{:S(2)}, u32[]{:S(2)}) collective-permute-start(f32[4,64,128]{2,1,0:T(8,128)S(1)} %get-tuple-element.54), channel_id=1, source_target_pairs={{0,8},{8,16},{16,24},{24,32},{32,40},{40,48},{48,56},{56,64},{64,7... | collective-permute-start | bytes 393224 | tf_op jit(solution)/shard_map/ppermute | solution.py:19
  152.5 8.3 %copy-start.5 = (f32[16,64,128]{2,1,0:T(8,128)S(1)}, f32[16,64,128]{2,1,0:T(8,128)}, u32[]{:S(2)}) copy-start(f32[16,64,128]{2,1,0:T(8,128)} %copy-done.4) | copy-start | bytes 1572868
  153.2 25.0 %collective-permute-start.8 = (f32[4,64,128]{2,1,0:T(8,128)}, f32[4,64,128]{2,1,0:T(8,128)S(1)}, u32[]{:S(2)}, u32[]{:S(2)}) collective-permute-start(f32[4,64,128]{2,1,0:T(8,128)} %get-tuple-element.62), channel_id=1, source_target_pairs={{8,0},{16,8},{24,16},{32,24},{40,32},{48,40},{56,48},{64,56},{72,6... | collective-permute-start | bytes 393224 | tf_op jit(solution)/shard_map/ppermute | solution.py:21
  154.5 23.8 %collective-permute-start.9 = (f32[4,64,128]{2,1,0:T(8,128)}, f32[4,64,128]{2,1,0:T(8,128)S(1)}, u32[]{:S(2)}, u32[]{:S(2)}) collective-permute-start(f32[4,64,128]{2,1,0:T(8,128)} %get-tuple-element.63), channel_id=1, source_target_pairs={{0,8},{8,16},{16,24},{24,32},{32,40},{40,48},{48,56},{56,64},{64,7... | collective-permute-start | bytes 393224 | tf_op jit(solution)/shard_map/ppermute | solution.py:19
  242.6 119.9 %copy-start.12 = (f32[16,8,128]{2,1,0:T(8,128)}, f32[16,8,128]{2,1,0:T(8,128)S(1)}, u32[]{:S(2)}) copy-start(f32[16,8,128]{2,1,0:T(8,128)S(1)} %broadcast_multiply_fusion) | copy-start | bytes 196612
  242.6 123.6 %copy-start.9 = (f32[2,5,16,8,128]{4,3,2,1,0:T(8,128)S(1)}, f32[2,5,16,8,128]{4,3,2,1,0:T(8,128)}, u32[]{:S(2)}) copy-start(f32[2,5,16,8,128]{4,3,2,1,0:T(8,128)} %param.25) | copy-start | bytes 1966084
  242.7 123.6 %copy-start.11 = (f32[16,8,128]{2,1,0:T(8,128)S(1)}, f32[16,8,128]{2,1,0:T(8,128)}, u32[]{:S(2)}) copy-start(f32[16,8,128]{2,1,0:T(8,128)} %reduce-scatter.2.cloned.1.call-done) | copy-start | bytes 196612
Sparse Core Ops, SparseCore 0:
  182.4 59.3 reduce-scatter.1
